TPU v7x, 32 devices: a whole 2x2x4 slice. The times are simulated.
32 devices in a mesh: src: 16 (over z, y, x), lev: 2 (over core).
Axes of the slice: x: 2, y: 2, z: 4, core: 2. Of those that a mesh axis runs over, the one named last changes fastest.
Arguments:
- field: bfloat16 [32768, 256], P('src', 'lev'), may hold values from -6 to 6
- grad_coef: float32 [2, 4, 32768], P(None, None, 'src'), may hold values from -6 to 6
- neighbours: int32 [32768, 4], P('src'), may hold values from 0 to 2175, as said below
- level_weight: float32 [8], replicated, may hold values from 0.2 to 2
- src_index: int32 [2048, 64], P('src'), may hold values from 0 to 2047
- tgt_index: int32 [2048, 32], P('src'), may hold values from 0 to 1023
- block_dest: int32 [2048, 1], P('src'), may hold values from 0 to 15; in each aligned block of 128 rows (0 to 127, 128 to 255, ...) at most 16 rows name the same one
- weights: bfloat16 [2048, 6144], P('src'), may hold values from -0.21875 to 0.21875
Outputs:
- remapped: bfloat16 [16384, 256], P('src', 'lev')
- column_total: float32 [32, 16384], P(None, 'src')
Inputs may be any that keep to these rules, and one draw needn't show every extreme that they name: `neighbours`: position 64 + p is the device's own cell p; positions below 64 and from 2112 on are the last and first cells of the devices before and after along the closed curve; a neighbour lies at most 64 cells from the cell. `block_dest`: the 128 blocks of one index of src name one target index at most 16 times.
All inputs are finite; a program needn't handle non-finite values.
Results may differ from a plain program's by a relative error of at most 0.0049.
Values may be sent and summed in bfloat16 or wider, within the bound.
A program may use at most 128 MiB of HBM per device.

v0:
```python
import jax
import jax.numpy as jnp
from jax import lax
from jax.sharding import PartitionSpec as P

FIELDS = 32
HW = 64
SB = 64
TB = 32
T_DEV = 1024


def extended_2(block, sides, width):
    for axis, dim in sides:
        count = lax.axis_size(axis)
        forward = [(i, i + 1) for i in range(count - 1)]
        forward.append((count - 1, 0))
        backward = [(target, source) for source, target in forward]
        low = lax.ppermute(
            lax.slice_in_dim(block, block.shape[dim] - width, None, axis=dim), axis, forward
        )
        high = lax.ppermute(lax.slice_in_dim(block, 0, width, axis=dim), axis, backward)
        block = jnp.concatenate([low, block, high], axis=dim)
    return block


def block_product(block_weights, block_rows):
    block_count = block_rows.shape[0]
    shaped = block_weights.reshape(block_count, 3 * SB, TB)
    return lax.dot_general(
        shaped, block_rows, (((1,), (1,)), ((0,), (0,))), preferred_element_type=jnp.float32
    )


def shards(field, grad_coef, neighbours, level_weight, src_index, tgt_index, block_dest, weights):
    extended = extended_2(field, (("src", 0),), HW)
    own_float = field.astype(jnp.float32)
    differ = extended[neighbours].astype(jnp.float32) - own_float[:, None, :]
    grad_east = jnp.sum(grad_coef[0].T[:, :, None] * differ, axis=1).astype(jnp.bfloat16)
    grad_north = jnp.sum(grad_coef[1].T[:, :, None] * differ, axis=1).astype(jnp.bfloat16)
    recon = jnp.stack([field, grad_east, grad_north])
    columns = field.shape[1]
    block_count = src_index.shape[0]
    block_rows = jnp.transpose(recon[:, src_index], (1, 0, 2, 3)).reshape(
        block_count, 3 * SB, columns
    )
    src_count = lax.axis_size("src")
    capacity = 2 * block_count // src_count
    target_owner = block_dest[:, 0]
    onehot = (target_owner[:, None] == jnp.arange(src_count, dtype=jnp.int32)[None, :]).astype(
        jnp.int32
    )
    before = jnp.cumsum(onehot, axis=0) - onehot
    slot_rank = jnp.sum(before * onehot, axis=1)
    slot_index = target_owner * capacity + slot_rank
    slots = src_count * capacity
    send_cells = jnp.zeros((slots, TB), jnp.int32).at[slot_index].set(tgt_index)
    recv_cells = lax.all_to_all(send_cells, "src", split_axis=0, concat_axis=0, tiled=True)
    partial_value = block_product(weights, block_rows)
    send_partial = jnp.zeros((slots, TB, columns), jnp.float32).at[slot_index].set(partial_value)
    received = lax.all_to_all(send_partial, "src", split_axis=0, concat_axis=0, tiled=True)
    total = (
        jnp.zeros((T_DEV, columns), jnp.float32)
        .at[recv_cells.reshape(-1)]
        .add(received.reshape(-1, columns))
    )
    remapped = total.astype(jnp.bfloat16)
    level_count = columns // FIELDS
    level_share = lax.dynamic_slice_in_dim(
        level_weight, lax.axis_index("lev") * level_count, level_count
    )
    local_sum = jnp.einsum(
        "tlf,l->ft",
        total.reshape(T_DEV, level_count, FIELDS),
        level_share,
        precision=lax.Precision.HIGHEST,
    )
    column_total = lax.psum(local_sum, "lev")
    return (remapped, column_total)


def solution(mesh):
    placed = (
        P("src", "lev"),
        P(None, None, "src"),
        P("src", None),
        P(),
        P("src", None),
        P("src", None),
        P("src", None),
        P("src", None),
    )
    return jax.shard_map(
        shards,
        mesh=mesh,
        in_specs=placed,
        out_specs=(P("src", "lev"), P(None, "src")),
        check_vma=False,
    )
```

profile of v0, /device:TPU:0, one launch (start us, length us, event | category | flops | bytes accessed | tf_op | source)
XLA Modules:
  0.0 406.4 jit_solution(9051789890176872774)
XLA Ops:
  8.0 3.0 collective-permute-start
  11.0 4.0 collective-permute-start.1
  19.8 3.5 all-to-all-start
  26.9 2.1 convert_element_type.40
  31.7 8.9 %copy.27 = bf16[1,2048,128]{2,0,1:T(2,128)(2,1)} copy(bf16[1,2048,128]{2,1,0:T(8,128)(2,1)S(1)} %bitcast.47) | data formatting | bytes 1048576 | tf_op jit(solution)/shard_map/stack | solution.py:41
  40.6 1.9 copy.32
  42.6 3.4 copy.33
  46.0 24.0 %gather_fusion = bf16[8192,128]{1,0:T(8,128)(2,1)S(1)} fusion(bf16[2176,128]{1,0:T(8,128)(2,1)S(1)} %pad_maximum_fusion.1, s32[8192]{0:T(1024)S(1)} %broadcast_clamp_fusion.1), kind=kCustom, calls=%fused_computation | custom fusion | bytes 4227072 | tf_op jit(solution)/shard_map/gather | solution.py:38
  70.0 15.1 %fusion.2 = (bf16[2048,128]{1,0:T(8,128)(2,1)S(1)}, bf16[2048,128]{1,0:T(8,128)(2,1)S(1)}) fusion(bf16[2048,4,128]{2,1,0:T(4,128)(2,1)S(1)} %bitcast.45, f32[2048,128]{1,0:T(8,128)} %convert_element_type.40, f32[2048,4]{1,0:T(8,128)} %copy.24, f32[2048,4]{1,0:T(8,128)} %copy.26), kind=kLoop, calls=%fused_computation.8 | loop fusion | flops 5767168 | bytes 4259840 | tf_op jit(solution)/shard_map/reduce_sum | solution.py:39
  85.1 8.3 %copy.28 = bf16[1,2048,128]{2,0,1:T(2,128)(2,1)S(1)} copy(bf16[1,2048,128]{2,1,0:T(8,128)(2,1)S(1)} %bitcast.50) | data formatting | bytes 1048576 | tf_op jit(solution)/shard_map/convert_element_type | solution.py:39
  93.4 8.1 %copy.29 = bf16[1,2048,128]{2,0,1:T(2,128)(2,1)S(1)} copy(bf16[1,2048,128]{2,1,0:T(8,128)(2,1)S(1)} %bitcast.49) | data formatting | bytes 1048576 | tf_op jit(solution)/shard_map/convert_element_type | solution.py:40
  101.6 3.6 pad_maximum_fusion
  105.1 56.5 %gather_fusion.1 = bf16[8192,3,128]{2,1,0:T(4,128)(2,1)} fusion(bf16[3,2048,128]{2,0,1:T(4,128)(2,1)S(1)} %pad_maximum_fusion, s32[8192]{0:T(1024)S(1)} %broadcast_clamp_fusion), kind=kCustom, calls=%fused_computation.1 | custom fusion | bytes 12615680 | tf_op jit(solution)/shard_map/gather | solution.py:44
  161.6 5.5 %copy.31 = bf16[128,3,64,128]{3,2,1,0:T(8,128)(2,1)S(1)} copy(bf16[128,3,64,128]{3,1,2,0:T(4,128)(2,1)} %bitcast.43) | data formatting | bytes 12582912 | tf_op jit(solution)/shard_map/transpose | solution.py:44
  167.1 2.4 convolution_bitcast_fusion
  169.5 2.5 broadcast_in_dim.24
  172.0 15.7 %scatter_fusion = f32[256,32,128]{2,1,0:T(8,128)} fusion(f32[256,32,128]{2,1,0:T(8,128)} %broadcast_in_dim.24, s32[128]{0:T(128)S(1)} %fusion.11, f32[128,32,128]{2,1,0:T(8,128)S(1)} %convolution_bitcast_fusion), kind=kCustom, calls=%fused_computation.3 | custom fusion | bytes 6291968 | tf_op jit(solution)/shard_map/scatter | solution.py:60
  187.7 6.9 %all-to-all-start.1 = ((f32[256,32,128]{2,1,0:T(8,128)}), f32[256,32,128]{2,1,0:T(8,128)}, u32[]{:S(2)}, u32[]{:S(2)}) async-start(f32[256,32,128]{2,1,0:T(8,128)} %scatter_fusion), calls=%async_computation.1 | async-start | bytes 8388608 | tf_op jit(solution)/shard_map/all_to_all | solution.py:61
  196.2 77.1 %all-to-all-done.1 = f32[256,32,128]{2,1,0:T(8,128)} async-done(((f32[256,32,128]{2,1,0:T(8,128)}), f32[256,32,128]{2,1,0:T(8,128)}, u32[]{:S(2)}, u32[]{:S(2)}) %all-to-all-start.1) | async-done | bytes 4194336 | tf_op jit(solution)/shard_map/all_to_all | solution.py:61
  273.3 53.3 %scatter_custom_fusion.2 = f32[1024,128]{1,0:T(8,128)S(1)} fusion(s32[8192]{0:T(1024)S(1)} %bitcast.53, f32[8192,128]{1,0:T(8,128)} %bitcast.18, f32[]{:T(128)} %constant.10.clone.1), kind=kCustom, calls=%fused_computation.17 | custom fusion | flops 1048576 | bytes 524800 | tf_op jit(solution)/shard_map/scatter-add | solution.py:65
  326.8 29.1 %fusion.4 = f32[1,1024,32]{0,1,2:T(8,128)} fusion(f32[1024,4,32]{0,2,1:T(8,128)S(1)} %bitcast.48, f32[8]{0:T(128)S(1)} %copy-done, s32[]{:T(128)S(6)} %select_n.28), kind=kOutput, calls=%fused_computation.13 | convolution fusion | flops 1572864 | bytes 655396 | tf_op jit(solution)/shard_map/tlf,l->ft/dot_general | solution.py:72
  356.0 10.6 %copy.36 = f32[1,1024,32]{1,2,0:T(8,128)} copy(f32[1,1024,32]{0,1,2:T(8,128)} %fusion.4) | data formatting | bytes 262144 | tf_op jit(solution)/shard_map/tlf,l->ft/dot_general | solution.py:72
  367.3 30.7 %all-reduce.2.cloned.1.call-done = f32[32,1024]{1,0:T(8,128)} async-done(((f32[32,1024]{1,0:T(8,128)}), f32[32,1024]{1,0:T(8,128)}) %all-reduce.2.cloned.1.call-update) | async-done | bytes 131088 | tf_op jit(solution)/shard_map/psum | solution.py:78
  398.0 1.6 copy.41
  (40 shorter events, 14.4 us)
Async XLA Ops:
  7.2 319.6 %copy-start = (f32[8]{0:T(128)S(1)}, f32[8]{0:T(128)}, u32[]{:S(2)}) copy-start(f32[8]{0:T(128)} %param.11) | copy-start | bytes 100
  7.2 24.6 %copy-start.2 = (bf16[2048,128]{1,0:T(8,128)(2,1)S(1)}, bf16[2048,128]{1,0:T(8,128)(2,1)}, u32[]{:S(2)}) copy-start(bf16[2048,128]{1,0:T(8,128)(2,1)} %param.8) | copy-start | bytes 1572868
  8.0 37.9 %collective-permute-start = (bf16[64,128]{1,0:T(8,128)(2,1)S(1)}, bf16[64,128]{1,0:T(8,128)(2,1)S(1)}, u32[]{:S(2)}, u32[]{:S(2)}) collective-permute-start(bf16[64,128]{1,0:T(8,128)(2,1)S(1)} %get-tuple-element.4), channel_id=1, source_target_pairs={{0,2},{2,4},{4,6},{6,8},{8,10},{10,12},{12,14},{14,16},{16,18},{18... | collective-permute-start | bytes 49160 | tf_op jit(solution)/shard_map/ppermute | solution.py:19
  11.0 35.0 %collective-permute-start.1 = (bf16[64,128]{1,0:T(8,128)(2,1)S(1)}, bf16[64,128]{1,0:T(8,128)(2,1)S(1)}, u32[]{:S(2)}, u32[]{:S(2)}) collective-permute-start(bf16[64,128]{1,0:T(8,128)(2,1)S(1)} %get-tuple-element.5), channel_id=1, source_target_pairs={{2,0},{4,2},{6,4},{8,6},{10,8},{12,10},{14,12},{16,14},{18,16},{20... | collective-permute-start | bytes 49160 | tf_op jit(solution)/shard_map/ppermute | solution.py:22
  19.8 167.9 %all-to-all-start = ((s32[16,1,512]{2,1,0:T(1,128)}), s32[16,1,512]{2,1,0:T(1,128)S(1)}, u32[]{:S(2)}, u32[]{:S(2)}) async-start(s32[16,1,512]{2,1,0:T(1,128)} %reshape.126), calls=%async_computation | async-start | bytes 65536 | tf_op jit(solution)/shard_map/all_to_all | solution.py:58
  70.0 31.5 %copy-start.3 = (bf16[1,2048,128]{2,0,1:T(2,128)(2,1)S(1)}, bf16[1,2048,128]{2,0,1:T(2,128)(2,1)}, u32[]{:S(2)}) copy-start(bf16[1,2048,128]{2,0,1:T(2,128)(2,1)} %copy.27) | copy-start | bytes 1572868
  161.6 5.5 %copy-start.1 = (bf16[128,192,32]{1,2,0:T(8,128)(2,1)S(1)}, bf16[128,192,32]{1,2,0:T(8,128)(2,1)}, u32[]{:S(2)}) copy-start(bf16[128,192,32]{1,2,0:T(8,128)(2,1)} %copy.33) | copy-start | bytes 4718596
  187.7 85.6 %all-to-all-start.1 = ((f32[256,32,128]{2,1,0:T(8,128)}), f32[256,32,128]{2,1,0:T(8,128)}, u32[]{:S(2)}, u32[]{:S(2)}) async-start(f32[256,32,128]{2,1,0:T(8,128)} %scatter_fusion), calls=%async_computation.1 | async-start | bytes 8388608 | tf_op jit(solution)/shard_map/all_to_all | solution.py:61
  194.7 203.3 %all-reduce.2.cloned.1.call-start = ((), (), s32[]{:S(2)}) async-start(), calls=%async_computation.2 | async-start | bytes 262144 | tf_op jit(solution)/shard_map/psum | solution.py:78
Sparse Core Ops, SparseCore 0:
  366.7 31.2 all-reduce.1
where the time goes:
time: 408 us; the launch traced here: 406 us
  local copies, waits for them, and re-layouts  156 us (38%)
  waiting for transfers between devices  108 us (26%)
  other arithmetic  79.5 us (19%)
  matrix products  31.6 us (8%)
  starting transfers between devices  17.4 us (4%)
  between operations  14.3 us (4%)
    all_to_all x1, waiting for transfers between devices, shards(): lax.all_to_all(send_partial, 'src', split_axis=0, concat_axis=0, tiled=True)  77.1 us
    gather x1, local copies, waits for them, and re-layouts, shards(): recon[:, src_index]  56.5 us
    scatter-add x1, other arithmetic, shards(): total = jnp.zeros((T_DEV, columns), jnp.float32).at[recv_cells.reshape(-1...  53.3 us
    psum x1, waiting for transfers between devices, shards(): column_total = lax.psum(local_sum, 'lev')  30.7 us
    dot_general x1, matrix products, shards(): jnp.einsum('tlf,l->ft', total.reshape(T_DEV, level_count, FIELDS), level_...  29.1 us
    gather x1, local copies, waits for them, and re-layouts, shards(): differ = extended[neighbours].astype(jnp.float32) - own_float[:, None, :]  24 us
    scatter x1, local copies, waits for them, and re-layouts, shards(): jnp.zeros((slots, TB, columns), jnp.float32).at[slot_index]  15.7 us
    reduce_sum x1, other arithmetic, shards(): jnp.sum(grad_coef[0].T[:, :, None] * differ, axis=1).astype(jnp.bfloat16)  15.1 us
  transfers between devices with their start and end apart: 5, of which 2 were waited for; matrix products, arithmetic and copies ran while one was open for 42% of the time, Pallas kernels for 0%

commit v1 on v0

--- a/solution.py
+++ b/solution.py
@@ -75,7 +75,7 @@
         level_share,
         precision=lax.Precision.HIGHEST,
     )
-    column_total = lax.psum(local_sum, "lev")
+    column_total = jnp.sum(lax.all_gather(local_sum, "lev"), axis=0)
     return (remapped, column_total)
 
 

time: 408 us -> 377 us (0.924)
  the two profiles are of different devices: /device:TPU:0 before, /device:TPU:17 now
where the time goes in v1:
time: 377 us; the launch traced here: 376 us
  local copies, waits for them, and re-layouts  154 us (41%)
  waiting for transfers between devices  89.6 us (24%)
  other arithmetic  81.2 us (22%)
  matrix products  31.3 us (8%)
  starting transfers between devices  15 us (4%)
  blocking collectives  4 us (1%)
    all_to_all x1, waiting for transfers between devices, shards(): lax.all_to_all(send_partial, 'src', split_axis=0, concat_axis=0, tiled=True)  89.6 us
    gather x1, local copies, waits for them, and re-layouts, shards(): recon[:, src_index]  56.5 us
    scatter-add x1, other arithmetic, shards(): total = jnp.zeros((T_DEV, columns), jnp.float32).at[recv_cells.reshape(-1...  54.4 us
    dot_general x1, matrix products, shards(): jnp.einsum('tlf,l->ft', total.reshape(T_DEV, level_count, FIELDS), level_...  28.9 us
    gather x1, local copies, waits for them, and re-layouts, shards(): differ = extended[neighbours].astype(jnp.float32) - own_float[:, None, :]  24 us
    scatter x1, local copies, waits for them, and re-layouts, shards(): jnp.zeros((slots, TB, columns), jnp.float32).at[slot_index]  15.7 us
    reduce_sum x1, other arithmetic, shards(): jnp.sum(grad_coef[0].T[:, :, None] * differ, axis=1).astype(jnp.bfloat16)  15.1 us
    dot_general x1, local copies, waits for them, and re-layouts, shards(): jnp.einsum('tlf,l->ft', total.reshape(T_DEV, level_count, FIELDS), level_...  9.95 us
  transfers between devices with their start and end apart: 4, of which 1 were waited for; matrix products, arithmetic and copies ran while one was open for 45% of the time, Pallas kernels for 0%

profile of v1, /device:TPU:17, one launch (start us, length us, event | category | flops | bytes accessed | tf_op | source)
XLA Modules:
  0.0 375.6 jit_solution(5238388410790337901)
XLA Ops:
  2.7 2.1 collective-permute-start.1
  9.6 5.3 %all-to-all-start = ((s32[16,1,512]{2,1,0:T(1,128)}), s32[16,1,512]{2,1,0:T(1,128)S(1)}, u32[]{:S(2)}, u32[]{:S(2)}) async-start(s32[16,1,512]{2,1,0:T(1,128)} %reshape.127), calls=%async_computation | async-start | bytes 65536 | tf_op jit(solution)/shard_map/all_to_all | solution.py:58
  18.5 2.1 convert_element_type.40
  20.6 1.4 copy.24
  22.0 1.4 copy.26
  23.3 8.9 %copy.27 = bf16[1,2048,128]{2,0,1:T(2,128)(2,1)} copy(bf16[1,2048,128]{2,1,0:T(8,128)(2,1)S(1)} %bitcast.48) | data formatting | bytes 1048576 | tf_op jit(solution)/shard_map/stack | solution.py:41
  32.2 1.9 copy.32
  34.1 3.4 copy.33
  37.6 24.0 %gather_fusion = bf16[8192,128]{1,0:T(8,128)(2,1)S(1)} fusion(bf16[2176,128]{1,0:T(8,128)(2,1)S(1)} %pad_maximum_fusion.1, s32[8192]{0:T(1024)S(1)} %broadcast_clamp_fusion.1), kind=kCustom, calls=%fused_computation | custom fusion | bytes 4227072 | tf_op jit(solution)/shard_map/gather | solution.py:38
  61.6 15.1 %fusion.2 = (bf16[2048,128]{1,0:T(8,128)(2,1)S(1)}, bf16[2048,128]{1,0:T(8,128)(2,1)S(1)}) fusion(bf16[2048,4,128]{2,1,0:T(4,128)(2,1)S(1)} %bitcast.46, f32[2048,128]{1,0:T(8,128)} %convert_element_type.40, f32[2048,4]{1,0:T(8,128)} %copy.24, f32[2048,4]{1,0:T(8,128)} %copy.26), kind=kLoop, calls=%fused_computation.8 | loop fusion | flops 5767168 | bytes 4259840 | tf_op jit(solution)/shard_map/reduce_sum | solution.py:39
  76.7 8.3 %copy.28 = bf16[1,2048,128]{2,0,1:T(2,128)(2,1)S(1)} copy(bf16[1,2048,128]{2,1,0:T(8,128)(2,1)S(1)} %bitcast.51) | data formatting | bytes 1048576 | tf_op jit(solution)/shard_map/convert_element_type | solution.py:39
  85.0 8.1 %copy.29 = bf16[1,2048,128]{2,0,1:T(2,128)(2,1)S(1)} copy(bf16[1,2048,128]{2,1,0:T(8,128)(2,1)S(1)} %bitcast.50) | data formatting | bytes 1048576 | tf_op jit(solution)/shard_map/convert_element_type | solution.py:40
  93.2 3.6 pad_maximum_fusion
  96.7 56.5 %gather_fusion.1 = bf16[8192,3,128]{2,1,0:T(4,128)(2,1)} fusion(bf16[3,2048,128]{2,0,1:T(4,128)(2,1)S(1)} %pad_maximum_fusion, s32[8192]{0:T(1024)S(1)} %broadcast_clamp_fusion), kind=kCustom, calls=%fused_computation.1 | custom fusion | bytes 12615680 | tf_op jit(solution)/shard_map/gather | solution.py:44
  153.2 5.5 %copy.31 = bf16[128,3,64,128]{3,2,1,0:T(8,128)(2,1)S(1)} copy(bf16[128,3,64,128]{3,1,2,0:T(4,128)(2,1)} %bitcast.44) | data formatting | bytes 12582912 | tf_op jit(solution)/shard_map/transpose | solution.py:44
  158.7 2.4 convolution_bitcast_fusion
  161.1 2.5 broadcast_in_dim.24
  163.6 15.7 %scatter_fusion = f32[256,32,128]{2,1,0:T(8,128)} fusion(f32[256,32,128]{2,1,0:T(8,128)} %broadcast_in_dim.24, s32[128]{0:T(128)S(1)} %fusion.11, f32[128,32,128]{2,1,0:T(8,128)S(1)} %convolution_bitcast_fusion), kind=kCustom, calls=%fused_computation.3 | custom fusion | bytes 6291968 | tf_op jit(solution)/shard_map/scatter | solution.py:60
  179.3 6.4 %all-to-all-start.1 = ((f32[256,32,128]{2,1,0:T(8,128)}), f32[256,32,128]{2,1,0:T(8,128)}, u32[]{:S(2)}, u32[]{:S(2)}) async-start(f32[256,32,128]{2,1,0:T(8,128)} %scatter_fusion), calls=%async_computation.1 | async-start | bytes 8388608 | tf_op jit(solution)/shard_map/all_to_all | solution.py:61
  187.2 89.6 %all-to-all-done.1 = f32[256,32,128]{2,1,0:T(8,128)} async-done(((f32[256,32,128]{2,1,0:T(8,128)}), f32[256,32,128]{2,1,0:T(8,128)}, u32[]{:S(2)}, u32[]{:S(2)}) %all-to-all-start.1) | async-done | bytes 4194336 | tf_op jit(solution)/shard_map/all_to_all | solution.py:61
  276.8 54.4 %scatter_custom_fusion.2 = f32[1024,128]{1,0:T(8,128)S(1)} fusion(s32[8192]{0:T(1024)S(1)} %bitcast.55, f32[8192,128]{1,0:T(8,128)} %bitcast.18, f32[]{:T(128)} %constant.10.clone.1), kind=kCustom, calls=%fused_computation.17 | custom fusion | flops 1048576 | bytes 524800 | tf_op jit(solution)/shard_map/scatter-add | solution.py:65
  332.1 28.9 %fusion.4 = f32[1,1024,32]{0,1,2:T(8,128)} fusion(f32[1024,4,32]{0,2,1:T(8,128)S(1)} %bitcast.49, f32[8]{0:T(128)S(1)} %copy-done, s32[]{:T(128)S(6)} %select_n.28), kind=kOutput, calls=%fused_computation.13 | convolution fusion | flops 1572864 | bytes 655396 | tf_op jit(solution)/shard_map/tlf,l->ft/dot_general | solution.py:72
  361.0 10.0 %copy.36 = f32[1,1024,32]{1,2,0:T(8,128)S(1)} copy(f32[1,1024,32]{0,1,2:T(8,128)} %fusion.4) | data formatting | bytes 262144 | tf_op jit(solution)/shard_map/tlf,l->ft/dot_general | solution.py:72
  370.9 4.0 %all-gather = f32[64,1024]{1,0:T(8,128)S(1)} all-gather(f32[32,1024]{1,0:T(8,128)S(1)} %bitcast.53), channel_id=2, replica_groups=mesh['src'=16,'lev'=2] {'lev'}, dimensions={0}, use_global_device_ids=true | all-gather | bytes 393216 | tf_op jit(solution)/shard_map/all_gather | solution.py:78
  (38 shorter events, 13.5 us)
Async XLA Ops:
  0.6 331.5 %copy-start = (f32[8]{0:T(128)S(1)}, f32[8]{0:T(128)}, u32[]{:S(2)}) copy-start(f32[8]{0:T(128)} %param.11) | copy-start | bytes 100
  0.6 22.7 %copy-start.2 = (bf16[2048,128]{1,0:T(8,128)(2,1)S(1)}, bf16[2048,128]{1,0:T(8,128)(2,1)}, u32[]{:S(2)}) copy-start(bf16[2048,128]{1,0:T(8,128)(2,1)} %param.8) | copy-start | bytes 1572868
  1.5 36.1 %collective-permute-start = (bf16[64,128]{1,0:T(8,128)(2,1)S(1)}, bf16[64,128]{1,0:T(8,128)(2,1)S(1)}, u32[]{:S(2)}, u32[]{:S(2)}) collective-permute-start(bf16[64,128]{1,0:T(8,128)(2,1)S(1)} %get-tuple-element.4), channel_id=1, source_target_pairs={{0,2},{2,4},{4,6},{6,8},{8,10},{10,12},{12,14},{14,16},{16,18},{18... | collective-permute-start | bytes 49160 | tf_op jit(solution)/shard_map/ppermute | solution.py:19
  2.7 34.9 %collective-permute-start.1 = (bf16[64,128]{1,0:T(8,128)(2,1)S(1)}, bf16[64,128]{1,0:T(8,128)(2,1)S(1)}, u32[]{:S(2)}, u32[]{:S(2)}) collective-permute-start(bf16[64,128]{1,0:T(8,128)(2,1)S(1)} %get-tuple-element.5), channel_id=1, source_target_pairs={{2,0},{4,2},{6,4},{8,6},{10,8},{12,10},{14,12},{16,14},{18,16},{20... | collective-permute-start | bytes 49160 | tf_op jit(solution)/shard_map/ppermute | solution.py:22
  9.6 169.7 %all-to-all-start = ((s32[16,1,512]{2,1,0:T(1,128)}), s32[16,1,512]{2,1,0:T(1,128)S(1)}, u32[]{:S(2)}, u32[]{:S(2)}) async-start(s32[16,1,512]{2,1,0:T(1,128)} %reshape.127), calls=%async_computation | async-start | bytes 65536 | tf_op jit(solution)/shard_map/all_to_all | solution.py:58
  61.6 31.5 %copy-start.3 = (bf16[1,2048,128]{2,0,1:T(2,128)(2,1)S(1)}, bf16[1,2048,128]{2,0,1:T(2,128)(2,1)}, u32[]{:S(2)}) copy-start(bf16[1,2048,128]{2,0,1:T(2,128)(2,1)} %copy.27) | copy-start | bytes 1572868
  153.2 5.5 %copy-start.1 = (bf16[128,192,32]{1,2,0:T(8,128)(2,1)S(1)}, bf16[128,192,32]{1,2,0:T(8,128)(2,1)}, u32[]{:S(2)}) copy-start(bf16[128,192,32]{1,2,0:T(8,128)(2,1)} %copy.33) | copy-start | bytes 4718596
  179.3 97.5 %all-to-all-start.1 = ((f32[256,32,128]{2,1,0:T(8,128)}), f32[256,32,128]{2,1,0:T(8,128)}, u32[]{:S(2)}, u32[]{:S(2)}) async-start(f32[256,32,128]{2,1,0:T(8,128)} %scatter_fusion), calls=%async_computation.1 | async-start | bytes 8388608 | tf_op jit(solution)/shard_map/all_to_all | solution.py:61
